TPU v7x, 128 devices: a whole 4x4x4 slice. The times are simulated.
128 devices in a mesh: node: 32 (over x, y, core), local: 4 (over z).
Axes of the slice: x: 4, y: 4, z: 4, core: 2. Of those that a mesh axis runs over, the one named last changes fastest.
Arguments:
- expert_ids: int32 [16384, 4], P(('node', 'local')), may hold values from 0 to 127, as said below
- gate_weights: bfloat16 [16384, 4], P(('node', 'local')), may hold values from 0.099609375 to 1
- tokens_in: bfloat16 [16384, 3584], P(('node', 'local')), may hold values from -6 to 6
- grad_out: bfloat16 [16384, 3584], P(('node', 'local')), may hold values from -6 to 6
- w_gate: bfloat16 [128, 3584, 1024], P(('node', 'local')), may hold values from -0.09375 to 0.09375
- w_up: bfloat16 [128, 3584, 1024], P(('node', 'local')), may hold values from -0.09375 to 0.09375
- w_down: bfloat16 [128, 1024, 3584], P(('node', 'local')), may hold values from -0.1875 to 0.1875
Outputs:
- grad_in: bfloat16 [16384, 3584], P(('node', 'local'))
Inputs may be any that keep to these rules, and one draw needn't show every extreme that they name: `expert_ids`: each token names 4 different experts, two in each of two different node groups; node group m holds experts 4 m to 4 m + 3. The tokens of one device pick every node group exactly 8 times. From the tokens of one device every expert gets at most 6 rows; in every node group one expert gets exactly 6 rows from every device, the others fewer, and every expert gets some rows.
All inputs are finite; a program needn't handle non-finite values.
Results may differ from a plain program's by a relative error of at most 0.0064.
Values may be sent and summed in bfloat16 or wider, within the bound.
A program may use at most 128 MiB of HBM per device.

v0:
```python
import jax
import jax.numpy as jnp
from jax import lax
from jax.sharding import PartitionSpec as P


def expert_rows(expert_x, expert_dy, gate_mat, up_mat, down_mat):
    pre_gate = jnp.dot(expert_x, gate_mat, preferred_element_type=jnp.float32)
    pre_up = jnp.dot(expert_x, up_mat, preferred_element_type=jnp.float32)
    grad_hidden = lax.dot_general(
        expert_dy, down_mat, (((1,), (1,)), ((), ())), preferred_element_type=jnp.float32
    )
    sigmoid_gate = jax.nn.sigmoid(pre_gate)
    grad_gate = (
        grad_hidden * pre_up * sigmoid_gate * (1.0 + pre_gate * (1.0 - sigmoid_gate))
    ).astype(jnp.bfloat16)
    grad_up = (grad_hidden * pre_gate * sigmoid_gate).astype(jnp.bfloat16)
    summed = lax.dot_general(
        grad_gate, gate_mat, (((1,), (1,)), ((), ())), preferred_element_type=jnp.float32
    )
    summed = summed + lax.dot_general(
        grad_up, up_mat, (((1,), (1,)), ((), ())), preferred_element_type=jnp.float32
    )
    return summed.astype(jnp.bfloat16)


def per_device(expert_ids, gate_weights, tokens_in, grad_out, w_gate, w_up, w_down):
    token_count = tokens_in.shape[0]
    feature_count = tokens_in.shape[1]
    node_count = lax.axis_size("node")
    local_count = lax.axis_size("local")
    expert_count = node_count * local_count
    visits = 2 * token_count // node_count
    slot_count = 3 * visits // 4
    gate_mat = w_gate[0]
    up_mat = w_up[0]
    down_mat = w_down[0]
    token_numbers = jnp.repeat(jnp.arange(token_count, dtype=jnp.int32), expert_ids.shape[1])
    onehot = jnp.sum(
        (expert_ids[:, :, None] == jnp.arange(expert_count, dtype=jnp.int32)).astype(jnp.int32),
        axis=1,
    )
    before = jnp.cumsum(onehot, axis=0) - onehot
    slot_rank = jnp.take_along_axis(before, expert_ids, axis=1)
    dest_row = expert_ids * slot_count + slot_rank
    owner_row = (
        jnp.zeros((expert_count * slot_count,), jnp.int32)
        .at[dest_row.reshape(-1)]
        .set(token_numbers + 1)
    )
    weight = (
        jnp.zeros((expert_count * slot_count,), jnp.float32)
        .at[dest_row.reshape(-1)]
        .set(gate_weights.reshape(-1).astype(jnp.float32))
    )
    present = owner_row > 0
    row_index = jnp.maximum(owner_row - 1, 0)
    send_x = jnp.where(present[:, None], tokens_in[row_index], jnp.zeros((), jnp.bfloat16))
    send_dy = (weight[:, None] * grad_out[row_index].astype(jnp.float32)).astype(jnp.bfloat16)
    send_x = send_x.reshape(expert_count, slot_count, feature_count)
    send_dy = send_dy.reshape(expert_count, slot_count, feature_count)
    part_x = lax.all_to_all(send_x, ("node", "local"), split_axis=0, concat_axis=0, tiled=True)
    part_dy = lax.all_to_all(send_dy, ("node", "local"), split_axis=0, concat_axis=0, tiled=True)
    pair_shape = part_x.shape
    done = expert_rows(
        part_x.reshape(-1, feature_count),
        part_dy.reshape(-1, feature_count),
        gate_mat,
        up_mat,
        down_mat,
    )
    done = done.reshape(pair_shape)
    returned = lax.all_to_all(done, ("node", "local"), split_axis=0, concat_axis=0, tiled=True)
    returned_rows = returned.reshape(expert_count * slot_count, feature_count)
    summed = jnp.sum(returned_rows[dest_row].astype(jnp.float32), axis=1)
    return summed.astype(jnp.bfloat16)


def solution(mesh):
    placed = (
        P(("node", "local"), None),
        P(("node", "local"), None),
        P(("node", "local"), None),
        P(("node", "local"), None),
        P(("node", "local"), None, None),
        P(("node", "local"), None, None),
        P(("node", "local"), None, None),
    )
    return jax.shard_map(
        per_device,
        mesh=mesh,
        in_specs=placed,
        out_specs=P(("node", "local"), None),
        check_vma=False,
    )
```

profile of v0, /device:TPU:1, one launch (start us, length us, event | category | flops | bytes accessed | tf_op | source)
XLA Modules:
  0.0 429.7 jit_solution(10414221108239473216)
XLA Ops:
  0.0 0.9 convert_reduce_fusion
  0.9 0.7 bitcast_or_fusion
  1.6 0.2 reduce_window_sum.11
  1.8 0.1 copy.26
  1.9 0.1 reshape.110
  2.0 0.0 copy-start.3
  2.0 3.6 gather_fusion.3
  5.7 0.1 reshape.113
  5.8 0.1 copy.27
  5.8 0.0 copy-done.3
  5.9 0.1 copy.28
  6.0 0.1 reshape.79
  6.1 0.1 reshape.128
  6.2 2.4 scatter_custom_fusion.1
  8.7 5.4 %gather_fusion.1 = bf16[768,3584]{1,0:T(8,128)(2,1)} fusion(bf16[128,3584]{1,0:T(8,128)(2,1)S(1)} %copy-done, s32[1024]{0:T(1024)S(1)} %pad_clamp_fusion.1), kind=kCustom, calls=%fused_computation.1 | custom fusion | bytes 11013120 | tf_op jit(solution)/shard_map/gather | solution.py:58
  14.1 9.6 %gather.18 = bf16[128,6,3584]{2,1,0:T(8,128)(2,1)} reshape(bf16[768,3584]{1,0:T(8,128)(2,1)} %gather_fusion.1) | data formatting | bytes 11010048 | tf_op jit(solution)/shard_map/gather | solution.py:58
  23.7 0.2 broadcast_in_dim.41
  23.8 6.8 %broadcast_select_fusion = bf16[128,6,3584]{2,1,0:T(8,128)(2,1)} fusion(bf16[128,6,3584]{2,1,0:T(8,128)(2,1)} %gather.18, pred[128,6]{1,0:T(8,128)(4,1)S(1)} %broadcast_in_dim.41), kind=kLoop, calls=%fused_computation.18 | loop fusion | flops 2752512 | bytes 11010816 | tf_op jit(solution)/shard_map/jit(_where)/select_n | solution.py:58
  30.6 11.9 %all-to-all-start.1 = ((bf16[128,6,3584]{2,1,0:T(8,128)(2,1)}), bf16[128,6,3584]{2,1,0:T(8,128)(2,1)}, u32[]{:S(2)}, u32[]{:S(2)}) async-start(bf16[128,6,3584]{2,1,0:T(8,128)(2,1)} %broadcast_select_fusion), calls=%async_computation.1 | async-start | bytes 14680064 | tf_op jit(solution)/shard_map/all_to_all | solution.py:62
  42.5 0.0 copy-done.2
  42.5 5.5 %gather_fusion = bf16[768,3584]{1,0:T(8,128)(2,1)} fusion(bf16[128,3584]{1,0:T(8,128)(2,1)S(1)} %copy-done.2, s32[1024]{0:T(1024)S(1)} %pad_clamp_fusion.1), kind=kCustom, calls=%fused_computation | custom fusion | bytes 11013120 | tf_op jit(solution)/shard_map/gather | solution.py:59
  48.0 10.2 %reshape.85 = f32[128,6,3584]{2,1,0:T(8,128)} reshape(bf16[768,3584]{1,0:T(8,128)(2,1)} %gather_fusion) | data formatting | bytes 16515072 | tf_op jit(solution)/shard_map/convert_element_type | solution.py:59
  58.2 0.1 copy.29
  58.3 0.1 reshape.120
  58.4 2.4 scatter_custom_fusion
  60.9 0.1 mul.37
  61.0 10.3 %multiply_convert_fusion = bf16[128,6,3584]{2,1,0:T(8,128)(2,1)} fusion(f32[128,6,3584]{2,1,0:T(8,128)} %reshape.85, f32[128,6]{1,0:T(8,128)S(1)} %mul.37), kind=kLoop, calls=%fused_computation.6 | loop fusion | flops 5505024 | bytes 16518144 | tf_op jit(solution)/shard_map/convert_element_type | solution.py:59
  71.4 59.1 %all-to-all-done.1 = bf16[128,6,3584]{2,1,0:T(8,128)(2,1)} async-done(((bf16[128,6,3584]{2,1,0:T(8,128)(2,1)}), bf16[128,6,3584]{2,1,0:T(8,128)(2,1)}, u32[]{:S(2)}, u32[]{:S(2)}) %all-to-all-start.1) | async-done | bytes 5505056 | tf_op jit(solution)/shard_map/all_to_all | solution.py:62
  130.5 11.6 %all-to-all-start = ((bf16[128,6,3584]{2,1,0:T(8,128)(2,1)}), bf16[128,6,3584]{2,1,0:T(8,128)(2,1)}, u32[]{:S(2)}, u32[]{:S(2)}) async-start(bf16[128,6,3584]{2,1,0:T(8,128)(2,1)} %multiply_convert_fusion), calls=%async_computation | async-start | bytes 14680064 | tf_op jit(solution)/shard_map/all_to_all | solution.py:63
  142.1 9.7 %reshape.81 = bf16[768,3584]{1,0:T(8,128)(2,1)} reshape(bf16[128,6,3584]{2,1,0:T(8,128)(2,1)} %all-to-all-done.1) | data formatting | bytes 11010048 | tf_op jit(solution)/shard_map/reshape | solution.py:66
  151.8 10.9 %fusion.2 = f32[768,1024]{1,0:T(8,128)} fusion(bf16[768,3584]{1,0:T(8,128)(2,1)} %reshape.81, bf16[1,3584,1024]{2,1,0:T(8,128)(2,1)} %param.11), kind=kOutput, calls=%fused_computation.10 | convolution fusion | flops 5637144576 | bytes 15990784 | tf_op jit(solution)/shard_map/dot_general | solution.py:8
  162.7 67.4 %all-to-all-done = bf16[128,6,3584]{2,1,0:T(8,128)(2,1)} async-done(((bf16[128,6,3584]{2,1,0:T(8,128)(2,1)}), bf16[128,6,3584]{2,1,0:T(8,128)(2,1)}, u32[]{:S(2)}, u32[]{:S(2)}) %all-to-all-start) | async-done | bytes 5505056 | tf_op jit(solution)/shard_map/all_to_all | solution.py:63
  230.0 9.8 %reshape.80 = bf16[768,3584]{1,0:T(8,128)(2,1)} reshape(bf16[128,6,3584]{2,1,0:T(8,128)(2,1)} %all-to-all-done) | data formatting | bytes 11010048 | tf_op jit(solution)/shard_map/reshape | solution.py:67
  239.8 9.9 %fusion.8 = f32[768,1024]{1,0:T(8,128)S(1)} fusion(bf16[768,3584]{1,0:T(8,128)(2,1)} %reshape.80, bf16[1,1024,3584]{2,1,0:T(8,128)(2,1)} %param.13), kind=kOutput, calls=%fused_computation.16 | convolution fusion | flops 5637144576 | bytes 15990784 | tf_op jit(solution)/shard_map/dot_general | solution.py:10
  249.7 1.6 copy-done.6
  251.3 0.0 slice-done.1
  251.4 8.8 %multiply_convert_fusion.2 = bf16[768,1024]{1,0:T(8,128)(2,1)S(1)} fusion(f32[768,1024]{1,0:T(8,128)S(1)} %copy-done.5, f32[768,1024]{1,0:T(8,128)S(1)} %fusion.8, bf16[768,3584]{1,0:T(8,128)(2,1)S(1)} %bitcast.27, bf16[1,3584,1024]{2,1,0:T(8,128)(2,1)} %param.12), kind=kOutput, calls=%fused_computation.20 | convolution fusion | flops 5645008896 | bytes 20709376 | tf_op jit(solution)/shard_map/dot_general | solution.py:9
  260.2 11.9 %fusion = f32[768,3584]{1,0:T(8,128)} fusion(bf16[768,1024]{1,0:T(8,128)(2,1)S(1)} %multiply_convert_fusion.2, bf16[1,3584,1024]{2,1,0:T(8,128)(2,1)} %param.11), kind=kOutput, calls=%fused_computation.8 | convolution fusion | flops 5637144576 | bytes 19922944 | tf_op jit(solution)/shard_map/dot_general | solution.py:18
  272.1 12.5 %add_convert_fusion = bf16[768,3584]{1,0:T(8,128)(2,1)} fusion(f32[768,3584]{1,0:T(8,128)} %fusion, bf16[1,3584,1024]{2,1,0:T(8,128)(2,1)} %param.12, f32[768,1024]{1,0:T(8,128)S(1)} %copy-done.7, f32[768,1024]{1,0:T(8,128)S(1)} %copy-done.5), kind=kOutput, calls=%fused_computation.7 | convolution fusion | flops 5647368192 | bytes 30146560 | tf_op jit(solution)/shard_map/dot_general | solution.py:21
  284.6 9.6 %reshape.82 = bf16[128,6,3584]{2,1,0:T(8,128)(2,1)} reshape(bf16[768,3584]{1,0:T(8,128)(2,1)} %add_convert_fusion) | data formatting | bytes 11010048 | tf_op jit(solution)/shard_map/reshape | solution.py:72
  294.1 12.3 %all-to-all-start.2 = ((bf16[128,6,3584]{2,1,0:T(8,128)(2,1)}), bf16[128,6,3584]{2,1,0:T(8,128)(2,1)}, u32[]{:S(2)}, u32[]{:S(2)}) async-start(bf16[128,6,3584]{2,1,0:T(8,128)(2,1)} %reshape.82), calls=%async_computation.2 | async-start | bytes 14680064 | tf_op jit(solution)/shard_map/all_to_all | solution.py:73
  306.4 0.1 copy.30
  306.6 0.1 reshape.104
  306.7 87.7 %all-to-all-done.2 = bf16[128,6,3584]{2,1,0:T(8,128)(2,1)} async-done(((bf16[128,6,3584]{2,1,0:T(8,128)(2,1)}), bf16[128,6,3584]{2,1,0:T(8,128)(2,1)}, u32[]{:S(2)}, u32[]{:S(2)}) %all-to-all-start.2) | async-done | bytes 5505056 | tf_op jit(solution)/shard_map/all_to_all | solution.py:73
  394.4 9.7 %reshape.83 = bf16[768,3584]{1,0:T(8,128)(2,1)} reshape(bf16[128,6,3584]{2,1,0:T(8,128)(2,1)} %all-to-all-done.2) | data formatting | bytes 11010048 | tf_op jit(solution)/shard_map/reshape | solution.py:74
  404.1 11.2 %gather_fusion.2 = bf16[512,3584]{1,0:T(8,128)(2,1)} fusion(bf16[768,3584]{1,0:T(8,128)(2,1)} %reshape.83, s32[1024]{0:T(1024)S(1)} %pad_clamp_fusion), kind=kCustom, calls=%fused_computation.2 | custom fusion | bytes 7342080 | tf_op jit(solution)/shard_map/gather | solution.py:75
  415.3 7.0 %reshape.107 = bf16[128,4,3584]{2,1,0:T(4,128)(2,1)} reshape(bf16[512,3584]{1,0:T(8,128)(2,1)} %gather_fusion.2) | data formatting | bytes 7340032 | tf_op jit(solution)/shard_map/gather | solution.py:75
  422.3 7.4 %reduce_sum.22 = bf16[128,3584]{1,0:T(8,128)(2,1)} reduce(bf16[128,4,3584]{2,1,0:T(4,128)(2,1)} %reshape.107, bf16[]{:T(256)} %constant.21.clone.1), dimensions={1}, to_apply=%region_4.5 | reduce | flops 1376256 | bytes 4587522 | tf_op jit(solution)/shard_map/reduce_sum | solution.py:75
  (24 shorter events, 0.1 us)
Async XLA Ops:
  0.0 8.7 %copy-start = (bf16[128,3584]{1,0:T(8,128)(2,1)S(1)}, bf16[128,3584]{1,0:T(8,128)(2,1)}, u32[]{:S(2)}) copy-start(bf16[128,3584]{1,0:T(8,128)(2,1)} %param.9) | copy-start | bytes 2752516
  2.0 3.8 copy-start.3
  30.6 11.9 %copy-start.2 = (bf16[128,3584]{1,0:T(8,128)(2,1)S(1)}, bf16[128,3584]{1,0:T(8,128)(2,1)}, u32[]{:S(2)}) copy-start(bf16[128,3584]{1,0:T(8,128)(2,1)} %param.10) | copy-start | bytes 2752516
  30.6 99.8 %all-to-all-start.1 = ((bf16[128,6,3584]{2,1,0:T(8,128)(2,1)}), bf16[128,6,3584]{2,1,0:T(8,128)(2,1)}, u32[]{:S(2)}, u32[]{:S(2)}) async-start(bf16[128,6,3584]{2,1,0:T(8,128)(2,1)} %broadcast_select_fusion), calls=%async_computation.1 | async-start | bytes 14680064 | tf_op jit(solution)/shard_map/all_to_all | solution.py:62
  48.0 10.2 %copy-start.4 = (bf16[128,4]{0,1:T(4,128)(2,1)S(1)}, bf16[128,4]{0,1:T(4,128)(2,1)}, u32[]{:S(2)}) copy-start(bf16[128,4]{0,1:T(4,128)(2,1)} %param.8) | copy-start | bytes 3076
  130.5 99.6 %all-to-all-start = ((bf16[128,6,3584]{2,1,0:T(8,128)(2,1)}), bf16[128,6,3584]{2,1,0:T(8,128)(2,1)}, u32[]{:S(2)}, u32[]{:S(2)}) async-start(bf16[128,6,3584]{2,1,0:T(8,128)(2,1)} %multiply_convert_fusion), calls=%async_computation | async-start | bytes 14680064 | tf_op jit(solution)/shard_map/all_to_all | solution.py:63
  230.0 21.3 %slice-start = ((s8[5505024]{0:T(1024)(128)(4,1)}), s8[1310720]{0:T(1024)(128)(4,1)S(1)}, s32[]{:S(2)}) async-start(s8[5505024]{0:T(1024)(128)(4,1)} %bitcast.26), calls=%async_computation.3 | async-start | bytes 2621440
  239.8 11.6 %slice-start.1 = ((s8[5505024]{0:T(1024)(128)(4,1)}), s8[4194304]{0:T(1024)(128)(4,1)S(1)}, s32[]{:S(2)}) async-start(s8[5505024]{0:T(1024)(128)(4,1)} %bitcast.26), calls=%async_computation.4 | async-start | bytes 8388608
  239.8 11.6 %copy-start.5 = (f32[768,1024]{1,0:T(8,128)S(1)}, f32[768,1024]{1,0:T(8,128)}, u32[]{:S(2)}) copy-start(f32[768,1024]{1,0:T(8,128)} %fusion.2) | copy-start | bytes 9437188
  249.7 1.6 copy-start.6
  260.2 11.9 %copy-start.7 = (f32[768,1024]{1,0:T(8,128)S(1)}, f32[768,1024]{1,0:T(8,128)}, u32[]{:S(2)}) copy-start(f32[768,1024]{1,0:T(8,128)} %copy-done.6) | copy-start | bytes 9437188
  294.1 100.2 %all-to-all-start.2 = ((bf16[128,6,3584]{2,1,0:T(8,128)(2,1)}), bf16[128,6,3584]{2,1,0:T(8,128)(2,1)}, u32[]{:S(2)}, u32[]{:S(2)}) async-start(bf16[128,6,3584]{2,1,0:T(8,128)(2,1)} %reshape.82), calls=%async_computation.2 | async-start | bytes 14680064 | tf_op jit(solution)/shard_map/all_to_all | solution.py:73
  404.1 25.7 %copy-start.1 = (bf16[128,3584]{1,0:T(8,128)(2,1)S(1)}, bf16[128,3584]{1,0:T(8,128)(2,1)}, u32[]{:S(2)}) copy-start(bf16[128,3584]{1,0:T(8,128)(2,1)} %param.9) | copy-start | bytes 2752516
where the time goes:
time: 437 us; the launch traced here: 430 us
  waiting for transfers between devices  214 us (49%)
  local copies, waits for them, and re-layouts  99.2 us (23%)
  matrix products  54 us (12%)
  starting transfers between devices  35.8 us (8%)
  other arithmetic  26.3 us (6%)
    all_to_all x1, waiting for transfers between devices, per_device(): lax.all_to_all(done, ('node', 'local'), split_axis=0, concat_axis=0, tile...  87.7 us
    all_to_all x1, waiting for transfers between devices, per_device(): lax.all_to_all(send_dy, ('node', 'local'), split_axis=0, concat_axis=0, t...  67.4 us
    all_to_all x1, waiting for transfers between devices, per_device(): lax.all_to_all(send_x, ('node', 'local'), split_axis=0, concat_axis=0, ti...  59.1 us
    gather x2, local copies, waits for them, and re-layouts, per_device(): summed = jnp.sum(returned_rows[dest_row].astype(jnp.float32), axis=1)  18.2 us
    gather x2, local copies, waits for them, and re-layouts, per_device(): tokens_in[row_index]  15 us
    dot_general x1, matrix products, expert_rows(): lax.dot_general(grad_up, up_mat, (((1,), (1,)), ((), ())), preferred_elem...  12.5 us
    all_to_all x1, starting transfers between devices, per_device(): lax.all_to_all(done, ('node', 'local'), split_axis=0, concat_axis=0, tile...  12.3 us
    dot_general x1, matrix products, expert_rows(): lax.dot_general(grad_gate, gate_mat, (((1,), (1,)), ((), ())), preferred_...  11.9 us
  transfers between devices with their start and end apart: 3, of which 3 were waited for; matrix products, arithmetic and copies ran while one was open for 12% of the time, Pallas kernels for 0%

commit v1 on v0

v1 whole, which is shorter than its diff:
```python
import functools

import jax
import jax.numpy as jnp
from jax import lax
from jax.experimental import pallas as pl
from jax.experimental.pallas import tpu as pltpu
from jax.sharding import PartitionSpec as P

MESH = pl.DeviceIdType.MESH
F32 = jnp.float32
BF16 = jnp.bfloat16

NX, NY, NC, NZ = 4, 4, 2, 4
NODES = NX * NY * NC
TOK = 128
D = 3584
FF = 1024
HALF = D // 2
META = 128
W = D + META
CH = 4
PER = NODES // CH
HPER = PER // 2
FR = 16
SLOT = 6
ROWS = NZ * PER * SLOT
VIS = NZ * PER * FR


def dot(a, b):
    return jnp.dot(a, b, preferred_element_type=F32)


def dot_nt(a, b):
    return lax.dot_general(a, b, (((1,), (1,)), ((), ())), preferred_element_type=F32)


def steps_of(i):
    dx = (i // 2) % 4
    dy = (dx + i // 8) % 4
    return dx, dy, i % 2


def node_plus(node, i):
    dx, dy, dc = steps_of(i)
    return ((node // 8 + dx) % 4) * 8 + (((node // 2) % 4 + dy) % 4) * 2 + (node + dc) % 2


def node_minus(node, i):
    dx, dy, dc = steps_of(i)
    return ((node // 8 + 4 - dx) % 4) * 8 + (((node // 2) % 4 + 4 - dy) % 4) * 2 + (node + dc) % 2


def kernel(
    ids_ref, wts_ref, x_hbm, g_hbm, wg_hbm, wu_hbm, wd_hbm, out_ref,
    wg, wu, wd, frames, visits, xd, gg, gu, sel01, selw, onehot,
    part, ring1, ring2, back, got,
    load_sem, xs, xr, h1s, h1r, h2s, h2r, r1s, r1r, r2s, r2r, bs, br,
):
    node = lax.axis_index("node")
    local = lax.axis_index("local")
    up = (local + 1) % 4
    down = (local + 3) % 4

    loads = [
        pltpu.make_async_copy(x_hbm, xd.at[pl.ds(0, TOK)], load_sem.at[0]),
        pltpu.make_async_copy(g_hbm, xd.at[pl.ds(TOK, TOK)], load_sem.at[1]),
        pltpu.make_async_copy(wg_hbm, wg, load_sem.at[2]),
        pltpu.make_async_copy(wu_hbm, wu, load_sem.at[3]),
        pltpu.make_async_copy(wd_hbm, wd, load_sem.at[4]),
    ]
    for load in loads:
        load.start()

    barrier = pltpu.get_barrier_semaphore()

    @pl.loop(1, NODES)
    def _(i):
        pl.semaphore_signal(barrier, 1, device_id=(node_plus(node, i), local), device_id_type=MESH)

    for z in (up, down):
        pl.semaphore_signal(barrier, 1, device_id=(node, z), device_id_type=MESH)

    ids = ids_ref[...]
    wts = wts_ref[...]
    target = node_plus(node, lax.broadcasted_iota(jnp.int32, (NODES, TOK), 0))
    names = jnp.zeros((NODES, TOK), F32)
    weights = [jnp.zeros((NODES, TOK), F32) for _ in range(NZ)]
    for k in range(4):
        expert = ids[k : k + 1, :]
        names = jnp.where(expert // 4 == target, 1.0, names)
        for z in range(NZ):
            weights[z] = weights[z] + jnp.where(expert == target * 4 + z, wts[k : k + 1, :], 0.0)
    earlier = lax.broadcasted_iota(jnp.int32, (TOK, TOK), 0) < lax.broadcasted_iota(jnp.int32, (TOK, TOK), 1)
    rank = dot(names.astype(BF16), earlier.astype(F32).astype(BF16))
    rank = jnp.where(names > 0.5, rank, -1.0)
    shape = (NODES, FR, TOK)
    place = lax.broadcasted_iota(jnp.int32, shape, 1)
    chosen = rank[:, None, :] == (place % 8).astype(F32)
    low = place < 8
    one_x = jnp.where(chosen & low, 1.0, 0.0).reshape(NODES * FR, TOK)
    one_g = jnp.where(chosen & ~low, 1.0, 0.0).reshape(NODES * FR, TOK)
    onehot[:, pl.ds(0, TOK)] = one_x.astype(BF16)
    onehot[:, pl.ds(TOK, TOK)] = one_g.astype(BF16)
    lane = lax.broadcasted_iota(jnp.int32, shape, 2)
    meta = jnp.zeros(shape, F32)
    for z in range(NZ):
        value = jnp.sum(jnp.where(chosen, weights[z][:, None, :], 0.0), axis=2, keepdims=True)
        meta = jnp.where(lane == z, value, meta)
    frames[:, :, pl.ds(D, META)] = meta.astype(BF16)

    loads[0].wait()
    loads[1].wait()
    pl.semaphore_wait(barrier, NODES + 1)

    def send(i):
        return pltpu.make_async_remote_copy(
            frames.at[i], visits.at[0, i], xs.at[i], xr.at[i],
            device_id=(node_plus(node, i), local), device_id_type=MESH,
        )

    @pl.loop(0, CH)
    def _(c):
        row = pl.multiple_of(c * PER * FR, PER * FR)

        @pl.loop(0, D // 512)
        def _(t):
            col = pl.multiple_of(t * 512, 512)
            block = dot(onehot[pl.ds(row, PER * FR), :], xd[pl.ds(0, 2 * TOK), pl.ds(col, 512)])
            frames[pl.ds(c * PER, PER), :, pl.ds(col, 512)] = block.astype(BF16).reshape(PER, FR, 512)

        @pl.loop(0, PER)
        def _(k):
            @pl.when(c * PER + k > 0)
            def _():
                send(c * PER + k).start()

    visits[0, 0] = frames[0]

    def hop1(c, way):
        peer, slot = ((up, 1), (down, 3))[way]
        return pltpu.make_async_remote_copy(
            visits.at[0, pl.ds(c * PER, PER)], visits.at[slot, pl.ds(c * PER, PER)],
            h1s.at[way, c], h1r.at[way, c], device_id=(node, peer), device_id_type=MESH,
        )

    def hop2(c, way):
        peer, slot = ((up, 1), (down, 3))[way]
        part_of = pl.ds(c * PER + way * HPER, HPER)
        return pltpu.make_async_remote_copy(
            visits.at[slot, part_of], visits.at[2, part_of],
            h2s.at[way, c], h2r.at[way, c], device_id=(node, peer), device_id_type=MESH,
        )

    def sum1(c, way):
        peer = (down, up)[way]
        return pltpu.make_async_remote_copy(
            part.at[c % 2, 2, pl.ds(way * HPER, HPER)], ring1.at[way, c],
            r1s.at[way, c], r1r.at[way, c], device_id=(node, peer), device_id_type=MESH,
        )

    def sum2(c, way):
        peer, slot = ((down, 1), (up, 3))[way]
        return pltpu.make_async_remote_copy(
            part.at[c % 2, slot], ring2.at[way, c],
            r2s.at[way, c], r2r.at[way, c], device_id=(node, peer), device_id_type=MESH,
        )

    def give(i):
        return pltpu.make_async_remote_copy(
            back.at[i], got.at[i], bs.at[i], br.at[i],
            device_id=(node_minus(node, i), local), device_id_type=MESH,
        )

    def select(c):
        info = visits[:, pl.ds(c * PER, PER), :, pl.ds(D, META)].reshape(VIS, META).astype(F32)
        lanes = lax.broadcasted_iota(jnp.int32, (VIS, META), 1)
        weight = jnp.sum(jnp.where(lanes == local, info, 0.0), axis=1, keepdims=True)
        mine = jnp.where(weight > 0.0, 1.0, 0.0)
        wide = jnp.broadcast_to(mine, (VIS, META)).astype(BF16)
        r = lax.broadcasted_iota(jnp.int32, (128, 128), 0)
        q = lax.broadcasted_iota(jnp.int32, (128, 128), 1)
        tri = jnp.where((r // 8 == q // 8) & (q < r), 1.0, 0.0).astype(BF16)
        ranks = jnp.concatenate(
            [dot(tri, wide[b * 128 : (b + 1) * 128]) for b in range(VIS // 128)], axis=0
        )
        ranks = jnp.where(mine > 0.5, ranks, -1.0)
        ranks = jnp.concatenate([ranks] * (2 * ROWS // META), axis=1)
        rr = lax.broadcasted_iota(jnp.int32, (VIS, 2 * ROWS), 0)
        cc = lax.broadcasted_iota(jnp.int32, (VIS, 2 * ROWS), 1)
        second = jnp.where(cc >= ROWS, 1, 0)
        cc = cc - ROWS * second
        frame = (cc * 171) >> 10
        slot = cc - 6 * frame
        hit = (ranks == slot.astype(F32)) & (rr // 8 == 2 * frame + second)
        ones = jnp.where(hit, 1.0, 0.0)
        sel01[...] = ones.astype(BF16)
        scaled = jnp.where(second == 1, ones * weight, ones)
        selw[...] = jnp.transpose(scaled).astype(BF16)

    def compute(c):
        select(c)

        @pl.loop(0, D // 512)
        def _(t):
            col = pl.multiple_of(t * 512, 512)
            block = visits[:, pl.ds(c * PER, PER), :, pl.ds(col, 512)].reshape(VIS, 512)
            xd[:, pl.ds(col, 512)] = dot(selw[...], block).astype(BF16)

        @pl.loop(0, FF // 256)
        def _(t):
            col = pl.multiple_of(t * 256, 256)
            pre_gate = dot(xd[pl.ds(0, ROWS), :], wg[:, pl.ds(col, 256)])
            pre_up = dot(xd[pl.ds(0, ROWS), :], wu[:, pl.ds(col, 256)])
            grad_hidden = dot_nt(xd[pl.ds(ROWS, ROWS), :], wd[pl.ds(col, 256), :])
            sig = 1.0 / (1.0 + jnp.exp(-pre_gate))
            gg[:, pl.ds(col, 256)] = (grad_hidden * pre_up * sig * (1.0 + pre_gate * (1.0 - sig))).astype(BF16)
            gu[:, pl.ds(col, 256)] = (grad_hidden * pre_gate * sig).astype(BF16)

        @pl.loop(0, HALF // 256)
        def _(t):
            col = pl.multiple_of(t * 256, 256)
            pieces = []
            for h in range(2):
                at = pl.ds(pl.multiple_of(h * HALF + t * 256, 256), 256)
                pieces.append((dot_nt(gg[...], wg[at, :]) + dot_nt(gu[...], wu[at, :])).astype(BF16))
            rows = jnp.concatenate(pieces, axis=0)
            block = dot(sel01[...], rows).astype(BF16)
            part[c % 2, :, :, :, pl.ds(col, 256)] = block.reshape(NZ, PER, FR, 256)

    @pl.loop(0, CH + 4)
    def _(s):
        @pl.when(s < CH)
        def _():
            @pl.loop(0, PER)
            def _(k):
                @pl.when(s * PER + k > 0)
                def _():
                    send(s * PER + k).wait_recv()

            hop1(s, 0).start()
            hop1(s, 1).start()

        @pl.when((s >= 1) & (s <= CH))
        def _():
            for way in range(2):
                hop1(s - 1, way).wait_recv()
                hop2(s - 1, way).start()

        @pl.when((s >= 3) & (s <= CH + 2))
        def _():
            c = s - 3
            for way in range(2):
                sum1(c, way).wait_recv()
                slot = (1, 3)[way]
                at = pl.ds(way * HPER, HPER)
                both = part[c % 2, slot, at].astype(F32) + ring1[way, c].astype(F32)
                part[c % 2, slot, at] = both.astype(BF16)
                sum2(c, way).start()

        @pl.when(s == 2)
        def _():
            for load in loads[2:]:
                load.wait()

        @pl.when(s >= 4)
        def _():
            c = s - 4
            for way in range(2):
                sum2(c, way).wait_recv()
            base = c * PER

            @pl.loop(0, PER)
            def _(k):
                total = part[c % 2, 0, k].astype(F32) + ring2[0, c, k].astype(F32) + ring2[1, c, k].astype(F32)
                back[base + k] = total.astype(BF16)

                @pl.when(base + k > 0)
                def _():
                    give(base + k).start()

        @pl.when((s >= 2) & (s <= CH + 1))
        def _():
            c = s - 2
            for way in range(2):
                hop2(c, way).wait_recv()

            @pl.when(c >= 2)
            def _():
                for way in range(2):
                    sum1(c - 2, way).wait_send()
                    sum2(c - 2, way).wait_send()

            compute(c)
            for way in range(2):
                sum1(c, way).start()

    got[0] = back[0]

    @pl.loop(1, NODES)
    def _(i):
        give(i).wait_recv()

    @pl.loop(0, HALF // 256)
    def _(t):
        col = pl.multiple_of(t * 256, 256)
        block = got[:, :, pl.ds(col, 256)].reshape(NODES * FR, 256)
        total = lax.dot_general(
            onehot[...], block, (((0,), (0,)), ((), ())), preferred_element_type=F32
        )
        out_ref[:, pl.ds(col, 256)] = total[:TOK].astype(BF16)
        out_ref[:, pl.ds(pl.multiple_of(HALF + t * 256, 256), 256)] = total[TOK:].astype(BF16)

    @pl.loop(1, NODES)
    def _(i):
        send(i).wait_send()
        give(i).wait_send()

    @pl.loop(0, CH)
    def _(c):
        for way in range(2):
            hop1(c, way).wait_send()
            hop2(c, way).wait_send()

    for c in range(CH - 2, CH):
        for way in range(2):
            sum1(c, way).wait_send()
            sum2(c, way).wait_send()


def per_device(expert_ids, gate_weights, tokens_in, grad_out, w_gate, w_up, w_down):
    ids = jnp.pad(expert_ids.T, ((0, 4), (0, 0)), constant_values=-1)
    wts = jnp.pad(gate_weights.astype(F32).T, ((0, 4), (0, 0)))
    vmem = pl.BlockSpec(memory_space=pltpu.VMEM)
    hbm = pl.BlockSpec(memory_space=pl.ANY)
    dma = pltpu.SemaphoreType.DMA
    return pl.pallas_call(
        kernel,
        out_shape=jax.ShapeDtypeStruct((TOK, D), BF16),
        in_specs=[vmem, vmem, hbm, hbm, hbm, hbm, hbm],
        out_specs=vmem,
        scratch_shapes=[
            pltpu.VMEM((D, FF), BF16),
            pltpu.VMEM((D, FF), BF16),
            pltpu.VMEM((FF, D), BF16),
            pltpu.VMEM((NODES, FR, W), BF16),
            pltpu.VMEM((NZ, NODES, FR, W), BF16),
            pltpu.VMEM((2 * ROWS, D), BF16),
            pltpu.VMEM((ROWS, FF), BF16),
            pltpu.VMEM((ROWS, FF), BF16),
            pltpu.VMEM((VIS, 2 * ROWS), BF16),
            pltpu.VMEM((2 * ROWS, VIS), BF16),
            pltpu.VMEM((NODES * FR, 2 * TOK), BF16),
            pltpu.VMEM((2, NZ, PER, FR, HALF), BF16),
            pltpu.VMEM((2, CH, HPER, FR, HALF), BF16),
            pltpu.VMEM((2, CH, PER, FR, HALF), BF16),
            pltpu.VMEM((NODES, FR, HALF), BF16),
            pltpu.VMEM((NODES, FR, HALF), BF16),
            dma((5,)),
            dma((NODES,)), dma((NODES,)),
            dma((2, CH)), dma((2, CH)), dma((2, CH)), dma((2, CH)),
            dma((2, CH)), dma((2, CH)), dma((2, CH)), dma((2, CH)),
            dma((NODES,)), dma((NODES,)),
        ],
        compiler_params=pltpu.CompilerParams(
            collective_id=0, has_side_effects=True, vmem_limit_bytes=65 * 1024 * 1024
        ),
    )(ids, wts, tokens_in, grad_out, w_gate[0], w_up[0], w_down[0])


def solution(mesh):
    placed = (
        P(("node", "local"), None),
        P(("node", "local"), None),
        P(("node", "local"), None),
        P(("node", "local"), None),
        P(("node", "local"), None, None),
        P(("node", "local"), None, None),
        P(("node", "local"), None, None),
    )
    return jax.shard_map(
        per_device,
        mesh=mesh,
        in_specs=placed,
        out_specs=P(("node", "local"), None),
        check_vma=False,
    )
```

time: 437 us -> 249 us (0.57); the launches traced: 430 us -> 249 us
  Pallas kernels: 0 us -> 244 us
  waiting for transfers between devices: 214 us -> 0 us
  local copies, waits for them, and re-layouts: 99.2 us -> 3.44 us
  matrix products: 54 us -> 0 us
  starting transfers between devices: 35.8 us -> 0 us
  other arithmetic: 26.3 us -> 1.27 us
    pallas_call x0 -> x1, Pallas kernels: none -> 244 us  [per_device(): pl.pallas_call(kernel, out_shape=jax.ShapeDtypeStruct((TOK, D), BF16), in...]
    all_to_all x3 -> x0, waiting for transfers between devices: 214 us -> none  [the longest x1 87.7 us: per_device(): lax.all_to_all(done, ('node', 'local'), split_axis=0, concat_axis=0, tile...]
    dot_general x5 -> x0, matrix products: 54 us -> none  [the longest x1 12.5 us: expert_rows(): lax.dot_general(grad_up, up_mat, (((1,), (1,)), ((), ())), preferred_elem...]
    gather x10 -> x0, local copies, waits for them, and re-layouts: 42.7 us -> none  [the longest x2 18.2 us: per_device(): summed = jnp.sum(returned_rows[dest_row].astype(jnp.float32), axis=1)]
    reshape x5 -> x0, local copies, waits for them, and re-layouts: 38.8 us -> none  [the longest x1 9.77 us: per_device(): part_dy.reshape(-1, feature_count)]
    all_to_all x3 -> x0, starting transfers between devices: 35.8 us -> none  [the longest x1 12.3 us: per_device(): lax.all_to_all(done, ('node', 'local'), split_axis=0, concat_axis=0, tile...]
    convert_element_type x3 -> x0, local copies, waits for them, and re-layouts: 10.5 us -> none  [the longest x1 10.2 us: per_device(): grad_out[row_index].astype(jnp.float32)]
    convert_element_type x1 -> x0, other arithmetic: 10.3 us -> none  [per_device(): (weight[:, None] * grad_out[row_index].astype(jnp.float32)).astype(jnp.bf...]
  transfers between devices with their start and end apart: 3 -> 0, of which waited for: 3 -> 0; matrix products, arithmetic and copies ran while one was open for 12% -> 0% of each run, Pallas kernels for 0% -> 0%
where the time goes in v1:
time: 249 us
  Pallas kernels  244 us (98%)
  local copies, waits for them, and re-layouts  3.44 us (1%)
    pallas_call x1, Pallas kernels, per_device(): pl.pallas_call(kernel, out_shape=jax.ShapeDtypeStruct((TOK, D), BF16), in...  244 us

profile of v1, /device:TPU:1, one launch (start us, length us, event | category | flops | bytes accessed | tf_op | source)
XLA Modules:
  0.0 248.9 jit_solution(11134419031381613949)
XLA Ops:
  0.0 1.3 pad.10.ids_ref
  1.3 1.3 pad_convert_fusion.wts_ref
  2.5 244.2 %shard_map.73 = bf16[128,3584]{1,0:T(8,128)(2,1)} custom-call(s32[8,128]{1,0:T(8,128)} %pad.10.ids_ref, f32[8,128]{1,0:T(8,128)} %pad_convert_fusion.wts_ref, bf16[128,3584]{1,0:T(8,128)(2,1)} %x_hbm.1, bf16[128,3584]{1,0:T(8,128)(2,1)} %g_hbm.1, bf16[3584,1024]{1,0:T(8,128)(2,1)} %bitcast.5, bf16[3584,1024]{1,0:T(8,128)(2,1)} %bitcast.6, ...), custom_call_target="tpu_custom_call" | custom-call | tf_op jit(solution)/shard_map/pallas_call | solution.py:338
  246.7 2.2 copy.9
